TPU v7x, 32 devices: a whole 2x2x4 slice. The times are simulated.
32 devices in a mesh: group: 2 (over y), seq: 4 (over z), tensor: 4 (over x, core).
Axes of the slice: x: 2, y: 2, z: 4, core: 2. Of those that a mesh axis runs over, the one named last changes fastest.
Arguments:
- spans: bfloat16 [1024, 3072], P(('group', 'seq')), parts along dimension 0, may hold values from -6 to 6
- w_in: bfloat16 [3072, 1024], P(None, 'tensor'), may hold values from -0.109375 to 0.109375
- band_weights: bfloat16 [4096, 128], P(('group', 'seq')), parts along dimension 0
- offsets: int32 [32], P(('group', 'seq')), parts along dimension 0, may hold values from 0 to 384, as said below
- w_up: bfloat16 [1024, 4096], P(None, 'tensor'), may hold values from -0.1875 to 0.1875
- d_up: bfloat16 [4096, 4096], P(('group', 'seq'), 'tensor'), parts along dimension 0, may hold values from -3 to 3
Outputs:
- up_proj: bfloat16 [4096, 4096], P(('group', 'seq'), 'tensor'), parts along dimension 0
- d_spans: bfloat16 [1024, 3072], P(('group', 'seq'), 'tensor'), parts along dimension 0
There are 2 independent parts, one for each index of `group`. A program takes and returns all parts, laid end to end along the dimension named above; an argument that names none is the same for every part. Nothing has to cross between parts.
Inputs may be any that keep to these rules, and one draw needn't show every extreme that they name: offsets[b] differs from b * 384 // 15 by at most 128, and both differences -128 and +128 occur in every draw; offsets[0] = 0 and offsets[15] = 384. Hence the bands of the bytes of seq index i lie within the span rows of seq indices i - 3 to i + 3.
All inputs are finite; a program needn't handle non-finite values.
Results may differ from a plain program's by a relative error of at most 0.0058.
Values may be sent and summed in bfloat16 or wider, within the bound.
No kernel may reach another device: no remote copies, remote signals or barrier semaphores. Data moves between devices by JAX's collectives and lax.ppermute only.
A program may use at most 64 MiB of HBM per device.

v0:
```python
import jax
import jax.numpy as jnp
from jax import lax
from jax.sharding import PartitionSpec as P


def band_matrix(band_weights, offsets, anchor, length):
    blocks = offsets.shape[0]
    breadth = band_weights.shape[1]
    band_cube = band_weights.reshape(blocks, -1, breadth)
    relative = anchor + jnp.arange(length, dtype=jnp.int32)[None, :] - offsets[:, None]
    picker = (relative[:, None, :] == jnp.arange(breadth, dtype=jnp.int32)[None, :, None]).astype(
        jnp.bfloat16
    )
    spread = jnp.einsum("bij,bjr->bir", band_cube, picker, preferred_element_type=jnp.float32)
    return spread.astype(jnp.bfloat16).reshape(-1, length)


def touches(offsets, breadth, anchor, length):
    return jnp.any((offsets < anchor + length) & (offsets + breadth > anchor))


def body(spans, w_in, band_weights, offsets, w_up, d_up):
    breadth = band_weights.shape[1]
    reduced = jnp.dot(spans, w_in, preferred_element_type=jnp.float32).astype(jnp.bfloat16)
    feature_count = reduced.shape[1]
    span_rows = reduced.shape[0]
    initial = jnp.zeros((band_weights.shape[0], feature_count), jnp.float32)
    shard_rows = lax.all_gather(reduced, "seq", axis=0, tiled=True)
    anchor = jnp.int32(0)
    length = shard_rows.shape[0]

    def accumulate(current):
        spread = band_matrix(band_weights, offsets, anchor, length)
        return jnp.dot(spread, shard_rows, preferred_element_type=jnp.float32)

    def unchanged(current):
        return current

    upsampled = lax.cond(
        touches(offsets, breadth, anchor, length), accumulate, unchanged, initial
    ).astype(jnp.bfloat16)
    gathered = lax.all_gather(upsampled, "tensor", axis=1, tiled=True)
    up_proj = jnp.dot(gathered, w_up, preferred_element_type=jnp.float32).astype(jnp.bfloat16)
    grad_cols = lax.psum_scatter(
        lax.dot_general(w_up, d_up, (((1,), (1,)), ((), ())), preferred_element_type=jnp.float32),
        "tensor",
        scatter_dimension=0,
        tiled=True,
    ).astype(jnp.bfloat16)

    def compute(operand):
        spread = band_matrix(band_weights, offsets, 0, span_rows * lax.axis_size("seq"))
        return lax.dot_general(
            spread, grad_cols, (((0,), (1,)), ((), ())), preferred_element_type=jnp.float32
        )

    def nothing(operand):
        return jnp.zeros((span_rows * lax.axis_size("seq"), feature_count), jnp.float32)

    every_row = lax.psum(
        lax.cond(
            touches(offsets, breadth, 0, span_rows * lax.axis_size("seq")), compute, nothing, 0
        ),
        "seq",
    )
    d_reduced = lax.dynamic_slice_in_dim(every_row, lax.axis_index("seq") * span_rows, span_rows, 0)
    d_reduced = d_reduced.astype(jnp.bfloat16)
    feature_parts = lax.dot_general(
        d_reduced, w_in, (((1,), (1,)), ((), ())), preferred_element_type=jnp.float32
    )
    d_spans = lax.psum_scatter(feature_parts, "tensor", scatter_dimension=1, tiled=True).astype(
        jnp.bfloat16
    )
    return (up_proj, d_spans)


def solution(mesh):
    placed = (
        P(("group", "seq"), None),
        P(None, "tensor"),
        P(("group", "seq"), None),
        P(("group", "seq")),
        P(None, "tensor"),
        P(("group", "seq"), "tensor"),
    )
    return jax.shard_map(
        body,
        mesh=mesh,
        in_specs=placed,
        out_specs=(P(("group", "seq"), "tensor"), P(("group", "seq"), "tensor")),
        check_vma=False,
    )
```

profile of v0, /device:TPU:0, one launch (start us, length us, event | category | flops | bytes accessed | tf_op | source)
XLA Modules:
  0.0 116.6 jit_solution(14578127177563211295)
XLA Ops:
  7.2 0.0 copy-start
  7.2 0.0 reduce-scatter.3.cloned.1.call-start
  7.2 1.5 %copy-done = bf16[1024,1024]{1,0:T(8,128)(2,1)S(1)} copy-done((bf16[1024,1024]{1,0:T(8,128)(2,1)S(1)}, bf16[1024,1024]{1,0:T(8,128)(2,1)}, u32[]{:S(2)}) %copy-start) | copy-done | bytes 2097176
  8.8 3.9 %fusion.6 = f32[1024,512]{1,0:T(8,128)} fusion(bf16[1024,1024]{1,0:T(8,128)(2,1)S(1)} %copy-done, bf16[512,1024]{1,0:T(8,128)(2,1)} %param.15), kind=kOutput, calls=%fused_computation.16 | convolution fusion | flops 1073741824 | bytes 5242880 | tf_op jit(solution)/shard_map/dot_general | solution.py:46
  12.6 0.0 reduce-scatter.3.cloned.1.call-update
  12.7 0.0 all-gather.2.cloned.1.call-start
  12.7 0.6 copy-done.4
  13.3 0.6 and_reduce_fusion
  14.6 0.0 copy-done.2
  14.6 1.8 %convolution_convert_fusion.3 = bf16[128,256]{1,0:T(8,128)(2,1)S(1)} fusion(bf16[128,3072]{1,0:T(8,128)(2,1)S(1)} %copy-done.2, bf16[3072,256]{1,0:T(8,128)(2,1)} %param.11), kind=kOutput, calls=%fused_computation.9 | convolution fusion | flops 201359360 | bytes 2424832 | tf_op jit(solution)/shard_map/dot_general | solution.py:25
  16.4 15.6 %all_gather.6 = bf16[512,256]{1,0:T(8,128)(2,1)S(1)} all-gather(bf16[128,256]{1,0:T(8,128)(2,1)S(1)} %convolution_convert_fusion.3), channel_id=1, replica_groups=mesh['group'=2,'seq'=4,'tensor'=4] {'seq'}, dimensions={0}, use_global_device_ids=true | all-gather | bytes 327680 | tf_op jit(solution)/shard_map/all_gather | solution.py:29
  32.0 0.7 conditional.2
  32.0 0.1 iota_subtract_fusion
  32.1 0.3 convolution_convert_fusion
  32.4 0.3 fusion.4
  32.7 0.0 copy-start.1
  32.7 0.7 copy-done.1
  33.4 0.0 all-gather.2.cloned.1.call-update
  33.5 0.0 reduce-scatter.5.cloned.1.call-start
  33.5 13.4 %reduce-scatter.3.cloned.1.call-done = f32[256,512]{1,0:T(8,128)} async-done(((f32[1024,512]{1,0:T(8,128)}), f32[256,512]{1,0:T(8,128)}) %reduce-scatter.3.cloned.1.call-update) | async-done | bytes 524304 | tf_op jit(solution)/shard_map/reduce_scatter | solution.py:45
  46.9 1.1 convert_element_type.40
  48.0 0.8 conditional.3
  48.0 0.1 iota_subtract_fusion.1
  48.1 0.3 convolution_convert_fusion.1
  48.5 0.3 fusion.5
  48.8 30.5 %all-reduce.1 = bf16[512,256]{1,0:T(8,128)(2,1)S(1)} all-reduce(f32[512,256]{1,0:T(8,128)S(1)} %get-tuple-element.27), channel_id=1, replica_groups=mesh['group'=2,'seq'=4,'tensor'=4] {'seq'}, use_global_device_ids=true, to_apply=%region_6.0 | all-reduce | flops 131072 | bytes 786432 | tf_op jit(solution)/shard_map/psum | solution.py:61
  79.3 3.2 %fusion.2 = f32[128,3072]{1,0:T(8,128)} fusion(bf16[3072,256]{1,0:T(8,128)(2,1)} %param.11, bf16[512,256]{1,0:T(8,128)(2,1)S(1)} %all-reduce.1, s32[]{:T(128)S(6)} %select_n.3), kind=kOutput, calls=%fused_computation.11 | convolution fusion | flops 201326592 | bytes 3211268 | tf_op jit(solution)/shard_map/dot_general | solution.py:69
  82.5 0.0 reduce-scatter.5.cloned.1.call-update
  82.5 0.0 all-gather.2.cloned.1.call-done
  82.5 3.4 %convolution_convert_fusion.2 = bf16[512,1024]{1,0:T(8,128)(2,1)} fusion(bf16[512,1024]{1,0:T(8,128)(2,1)} %all-gather.2.cloned.1.call-done, bf16[1024,1024]{1,0:T(8,128)(2,1)S(1)} %copy-done), kind=kOutput, calls=%fused_computation.8 | convolution fusion | flops 1074266112 | bytes 4194304 | tf_op jit(solution)/shard_map/dot_general | solution.py:44
  86.0 22.4 %reduce-scatter.5.cloned.1.call-done = f32[128,768]{1,0:T(8,128)} async-done(((f32[128,3072]{1,0:T(8,128)}), f32[128,768]{1,0:T(8,128)}) %reduce-scatter.5.cloned.1.call-update) | async-done | bytes 393232 | tf_op jit(solution)/shard_map/reduce_scatter | solution.py:72
  108.4 1.7 %convert_element_type.42 = bf16[128,768]{1,0:T(8,128)(2,1)} convert(f32[128,768]{1,0:T(8,128)} %reduce-scatter.5.cloned.1.call-done) | non-fusion elementwise | flops 98304 | bytes 589824 | tf_op jit(solution)/shard_map/convert_element_type | solution.py:72
  (4 shorter events, 0.0 us)
Async XLA Ops:
  7.2 1.6 %copy-start = (bf16[1024,1024]{1,0:T(8,128)(2,1)S(1)}, bf16[1024,1024]{1,0:T(8,128)(2,1)}, u32[]{:S(2)}) copy-start(bf16[1024,1024]{1,0:T(8,128)(2,1)} %param.14) | copy-start | bytes 6291460
  7.2 39.8 %reduce-scatter.3.cloned.1.call-start = ((), (), s32[]{:S(2)}) async-start(), calls=%async_computation.3 | async-start | bytes 2621440 | tf_op jit(solution)/shard_map/reduce_scatter | solution.py:45
  12.6 0.7 copy-start.4
  12.6 1.9 %copy-start.2 = (bf16[128,3072]{1,0:T(8,128)(2,1)S(1)}, bf16[128,3072]{1,0:T(8,128)(2,1)}, u32[]{:S(2)}) copy-start(bf16[128,3072]{1,0:T(8,128)(2,1)} %param.10) | copy-start | bytes 2359300
  12.6 19.4 %copy-start.3 = (bf16[512,128]{1,0:T(8,128)(2,1)S(1)}, bf16[512,128]{1,0:T(8,128)(2,1)}, u32[]{:S(2)}) copy-start(bf16[512,128]{1,0:T(8,128)(2,1)} %param.12) | copy-start | bytes 393220
  12.7 69.9 %all-gather.2.cloned.1.call-start = ((), (), s32[]{:S(2)}) async-start(), calls=%async_computation.2 | async-start | bytes 1310720 | tf_op jit(solution)/shard_map/all_gather | solution.py:43
  32.7 0.7 copy-start.1
  33.5 74.9 %reduce-scatter.5.cloned.1.call-start = ((), (), s32[]{:S(2)}) async-start(), calls=%async_computation.4 | async-start | bytes 1966080 | tf_op jit(solution)/shard_map/reduce_scatter | solution.py:72
Sparse Core Ops, SparseCore 0:
  12.8 34.1 reduce-scatter.2
  49.1 16.8 all-gather.1
  82.6 25.7 reduce-scatter.4
where the time goes:
time: 117 us
  blocking collectives  46.1 us (39%)
  waiting for transfers between devices  35.9 us (31%)
  between operations  14.5 us (12%)
  matrix products  13.6 us (12%)
  other arithmetic  3.54 us (3%)
  local copies, waits for them, and re-layouts  2.83 us (2%)
    psum x1, blocking collectives, body(): lax.psum(lax.cond(touches(offsets, breadth, 0, span_rows * lax.axis_size(...  30.5 us
    reduce_scatter x1, waiting for transfers between devices, body(): lax.psum_scatter(feature_parts, 'tensor', scatter_dimension=1, tiled=True)  22.4 us
    all_gather x1, blocking collectives, body(): shard_rows = lax.all_gather(reduced, 'seq', axis=0, tiled=True)  15.6 us
    reduce_scatter x1, waiting for transfers between devices, body(): lax.psum_scatter(lax.dot_general(w_up, d_up, (((1,), (1,)), ((), ())), pr...  13.4 us
    dot_general x1, matrix products, body(): lax.dot_general(w_up, d_up, (((1,), (1,)), ((), ())), preferred_element_t...  3.86 us
    dot_general x1, matrix products, body(): jnp.dot(gathered, w_up, preferred_element_type=jnp.float32)  3.45 us
    dot_general x1, matrix products, body(): lax.dot_general(d_reduced, w_in, (((1,), (1,)), ((), ())), preferred_elem...  3.22 us
    unnamed x10, local copies, waits for them, and re-layouts  2.83 us
  transfers between devices with their start and end apart: 3, of which 2 were waited for; matrix products, arithmetic and copies ran while one was open for 10% of the time, Pallas kernels for 0%

commit v1 on v0

--- a/solution.py
+++ b/solution.py
@@ -2,6 +2,21 @@
 import jax.numpy as jnp
 from jax import lax
 from jax.sharding import PartitionSpec as P
+
+
+def follow_signs(local_array):
+    n_slots = lax.axis_size("seq")
+    cards = [local_array]
+    for dev_j in tuple(range(n_slots - 1)):
+        cards.append(
+            lax.ppermute(cards[-1], "seq", [(dd, (dd + 1) % n_slots) for dd in range(n_slots)])
+        )
+    field_out = jnp.roll(
+        jnp.concatenate(cards[::-1], axis=0),
+        (lax.axis_index("seq") + 1) * local_array.shape[0],
+        axis=0,
+    )
+    return field_out
 
 
 def band_matrix(band_weights, offsets, anchor, length):
@@ -26,7 +41,7 @@
     feature_count = reduced.shape[1]
     span_rows = reduced.shape[0]
     initial = jnp.zeros((band_weights.shape[0], feature_count), jnp.float32)
-    shard_rows = lax.all_gather(reduced, "seq", axis=0, tiled=True)
+    shard_rows = follow_signs(reduced)
     anchor = jnp.int32(0)
     length = shard_rows.shape[0]
 

time: 117 us -> 117 us (level)
  blocking collectives: 46.1 us -> 30.3 us
  waiting for transfers between devices: 35.9 us -> 48 us
  starting transfers between devices: 0.12 us -> 3.2 us
    all_gather x1 -> x0, blocking collectives: 15.6 us -> none  [body(): shard_rows = lax.all_gather(reduced, 'seq', axis=0, tiled=True)]
    ppermute x0 -> x3, waiting for transfers between devices: none -> 15.1 us  [follow_signs(): lax.ppermute(cards[-1], 'seq', [(dd, (dd + 1) % n_slots) for dd in range(...]
    reduce_scatter x1, waiting for transfers between devices: 13.4 us -> 10.2 us  [body(): lax.psum_scatter(lax.dot_general(w_up, d_up, (((1,), (1,)), ((), ())), pr...]
    ppermute x0 -> x3, starting transfers between devices: none -> 3.08 us  [follow_signs(): lax.ppermute(cards[-1], 'seq', [(dd, (dd + 1) % n_slots) for dd in range(...]
    unnamed x10 -> x17, local copies, waits for them, and re-layouts: 2.83 us -> 3.34 us
  transfers between devices with their start and end apart: 3 -> 6, of which waited for: 2 -> 5; matrix products, arithmetic and copies ran while one was open for 10% -> 10% of each run, Pallas kernels for 0% -> 0%
where the time goes in v1:
time: 117 us
  waiting for transfers between devices  48 us (41%)
  blocking collectives  30.3 us (26%)
  between operations  14.5 us (12%)
  matrix products  13.6 us (12%)
  other arithmetic  3.54 us (3%)
  local copies, waits for them, and re-layouts  3.35 us (3%)
  starting transfers between devices  3.2 us (3%)
    psum x1, blocking collectives, body(): lax.psum(lax.cond(touches(offsets, breadth, 0, span_rows * lax.axis_size(...  30.3 us
    reduce_scatter x1, waiting for transfers between devices, body(): lax.psum_scatter(feature_parts, 'tensor', scatter_dimension=1, tiled=True)  22.6 us
    ppermute x3, waiting for transfers between devices, follow_signs(): lax.ppermute(cards[-1], 'seq', [(dd, (dd + 1) % n_slots) for dd in range(...  15.1 us
    reduce_scatter x1, waiting for transfers between devices, body(): lax.psum_scatter(lax.dot_general(w_up, d_up, (((1,), (1,)), ((), ())), pr...  10.2 us
    dot_general x1, matrix products, body(): lax.dot_general(w_up, d_up, (((1,), (1,)), ((), ())), preferred_element_t...  3.85 us
    dot_general x1, matrix products, body(): jnp.dot(gathered, w_up, preferred_element_type=jnp.float32)  3.45 us
    unnamed x17, local copies, waits for them, and re-layouts  3.34 us
    dot_general x1, matrix products, body(): lax.dot_general(d_reduced, w_in, (((1,), (1,)), ((), ())), preferred_elem...  3.21 us
  transfers between devices with their start and end apart: 6, of which 5 were waited for; matrix products, arithmetic and copies ran while one was open for 10% of the time, Pallas kernels for 0%

profile of v1, /device:TPU:0, one launch (start us, length us, event | category | flops | bytes accessed | tf_op | source)
XLA Modules:
  0.0 116.6 jit_solution(1669245863912609860)
XLA Ops:
  7.2 0.0 reduce-scatter.3.cloned.1.call-start
  7.2 1.5 %copy-done = bf16[1024,1024]{1,0:T(8,128)(2,1)S(1)} copy-done((bf16[1024,1024]{1,0:T(8,128)(2,1)S(1)}, bf16[1024,1024]{1,0:T(8,128)(2,1)}, u32[]{:S(2)}) %copy-start) | copy-done | bytes 2097176
  8.8 3.8 %fusion.8 = f32[1024,512]{1,0:T(8,128)} fusion(bf16[1024,1024]{1,0:T(8,128)(2,1)S(1)} %copy-done, bf16[512,1024]{1,0:T(8,128)(2,1)} %param.15), kind=kOutput, calls=%fused_computation.26 | convolution fusion | flops 1073741824 | bytes 5242880 | tf_op jit(solution)/shard_map/dot_general | solution.py:61
  12.6 0.0 reduce-scatter.3.cloned.1.call-update
  12.7 0.0 all-gather.2.cloned.1.call-start
  12.7 1.0 copy-done.2
  13.7 1.8 %convolution_convert_fusion.3 = bf16[128,256]{1,0:T(8,128)(2,1)S(1)} fusion(bf16[128,3072]{1,0:T(8,128)(2,1)S(1)} %copy-done.2, bf16[3072,256]{1,0:T(8,128)(2,1)} %param.11), kind=kOutput, calls=%fused_computation.12 | convolution fusion | flops 201359360 | bytes 2424832 | tf_op jit(solution)/shard_map/dot_general | solution.py:40
  15.5 3.1 %collective-permute-start = (bf16[128,256]{1,0:T(8,128)(2,1)S(1)}, bf16[128,256]{1,0:T(8,128)(2,1)S(1)}, u32[]{:S(2)}, u32[]{:S(2)}) collective-permute-start(bf16[128,256]{1,0:T(8,128)(2,1)S(1)} %convolution_convert_fusion.3), channel_id=1, source_target_pairs={{0,4},{4,8},{8,12},{12,0},{1,5},{5,9},{9,13},{13,1},{2,6},{6,10},{... | collective-permute-start | bytes 196616 | tf_op jit(solution)/shard_map/ppermute | solution.py:12
  18.6 4.3 %collective-permute-done = bf16[128,256]{1,0:T(8,128)(2,1)S(1)} collective-permute-done((bf16[128,256]{1,0:T(8,128)(2,1)S(1)}, bf16[128,256]{1,0:T(8,128)(2,1)S(1)}, u32[]{:S(2)}, u32[]{:S(2)}) %collective-permute-start) | collective-permute-done | bytes 65568 | tf_op jit(solution)/shard_map/ppermute | solution.py:12
  22.9 6.1 %collective-permute-done.1 = bf16[128,256]{1,0:T(8,128)(2,1)S(1)} collective-permute-done((bf16[128,256]{1,0:T(8,128)(2,1)S(1)}, bf16[128,256]{1,0:T(8,128)(2,1)S(1)}, u32[]{:S(2)}, u32[]{:S(2)}) %collective-permute-start.1) | collective-permute-done | bytes 65568 | tf_op jit(solution)/shard_map/ppermute | solution.py:12
  29.0 0.6 and_reduce_fusion
  30.2 4.8 %collective-permute-done.2 = bf16[128,256]{1,0:T(8,128)(2,1)S(1)} collective-permute-done((bf16[128,256]{1,0:T(8,128)(2,1)S(1)}, bf16[128,256]{1,0:T(8,128)(2,1)S(1)}, u32[]{:S(2)}, u32[]{:S(2)}) %collective-permute-start.2) | collective-permute-done | bytes 65568 | tf_op jit(solution)/shard_map/ppermute | solution.py:12
  35.1 0.8 conditional.2
  35.2 0.1 iota_subtract_fusion.1
  35.2 0.3 convolution_convert_fusion.1
  35.6 0.3 fusion.2
  35.9 0.7 copy-done.1
  36.6 0.0 all-gather.2.cloned.1.call-update
  36.6 0.0 reduce-scatter.5.cloned.1.call-start
  36.7 10.2 %reduce-scatter.3.cloned.1.call-done = f32[256,512]{1,0:T(8,128)} async-done(((f32[1024,512]{1,0:T(8,128)}), f32[256,512]{1,0:T(8,128)}) %reduce-scatter.3.cloned.1.call-update) | async-done | bytes 524304 | tf_op jit(solution)/shard_map/reduce_scatter | solution.py:60
  46.9 1.1 convert_element_type.40
  48.0 0.8 conditional.3
  48.0 0.1 iota_subtract_fusion
  48.1 0.3 convolution_convert_fusion
  48.4 0.3 fusion.7
  48.8 30.3 %all-reduce.1 = bf16[512,256]{1,0:T(8,128)(2,1)S(1)} all-reduce(f32[512,256]{1,0:T(8,128)S(1)} %get-tuple-element.52), channel_id=1, replica_groups=mesh['group'=2,'seq'=4,'tensor'=4] {'seq'}, use_global_device_ids=true, to_apply=%region_6.7 | all-reduce | flops 131072 | bytes 786432 | tf_op jit(solution)/shard_map/psum | solution.py:76
  79.1 3.2 %fusion.5 = f32[128,3072]{1,0:T(8,128)} fusion(bf16[3072,256]{1,0:T(8,128)(2,1)} %param.11, bf16[512,256]{1,0:T(8,128)(2,1)S(1)} %all-reduce.1, s32[]{:T(128)S(6)} %select_n.18), kind=kOutput, calls=%fused_computation.14 | convolution fusion | flops 201326592 | bytes 3211268 | tf_op jit(solution)/shard_map/dot_general | solution.py:84
  82.3 0.0 reduce-scatter.5.cloned.1.call-update
  82.3 0.0 all-gather.2.cloned.1.call-done
  82.3 3.4 %convolution_convert_fusion.2 = bf16[512,1024]{1,0:T(8,128)(2,1)} fusion(bf16[512,1024]{1,0:T(8,128)(2,1)} %all-gather.2.cloned.1.call-done, bf16[1024,1024]{1,0:T(8,128)(2,1)S(1)} %copy-done), kind=kOutput, calls=%fused_computation.11 | convolution fusion | flops 1074266112 | bytes 4194304 | tf_op jit(solution)/shard_map/dot_general | solution.py:59
  85.8 22.6 %reduce-scatter.5.cloned.1.call-done = f32[128,768]{1,0:T(8,128)} async-done(((f32[128,3072]{1,0:T(8,128)}), f32[128,768]{1,0:T(8,128)}) %reduce-scatter.5.cloned.1.call-update) | async-done | bytes 393232 | tf_op jit(solution)/shard_map/reduce_scatter | solution.py:87
  108.4 1.7 %convert_element_type.42 = bf16[128,768]{1,0:T(8,128)(2,1)} convert(f32[128,768]{1,0:T(8,128)} %reduce-scatter.5.cloned.1.call-done) | non-fusion elementwise | flops 98304 | bytes 589824 | tf_op jit(solution)/shard_map/convert_element_type | solution.py:87
  (17 shorter events, 0.1 us)
Async XLA Ops:
  7.2 1.6 %copy-start = (bf16[1024,1024]{1,0:T(8,128)(2,1)S(1)}, bf16[1024,1024]{1,0:T(8,128)(2,1)}, u32[]{:S(2)}) copy-start(bf16[1024,1024]{1,0:T(8,128)(2,1)} %param.14) | copy-start | bytes 6291460
  7.2 39.8 %reduce-scatter.3.cloned.1.call-start = ((), (), s32[]{:S(2)}) async-start(), calls=%async_computation.3 | async-start | bytes 2621440 | tf_op jit(solution)/shard_map/reduce_scatter | solution.py:60
  12.6 1.1 copy-start.2
  12.6 16.3 %copy-start.4 = (s32[4]{0:T(128)S(1)}, s32[4]{0:T(128)}, u32[]{:S(2)}) copy-start(s32[4]{0:T(128)} %param.13) | copy-start | bytes 52
  12.6 22.5 %copy-start.3 = (bf16[512,128]{1,0:T(8,128)(2,1)S(1)}, bf16[512,128]{1,0:T(8,128)(2,1)}, u32[]{:S(2)}) copy-start(bf16[512,128]{1,0:T(8,128)(2,1)} %param.12) | copy-start | bytes 393220
  12.7 69.7 %all-gather.2.cloned.1.call-start = ((), (), s32[]{:S(2)}) async-start(), calls=%async_computation.2 | async-start | bytes 1310720 | tf_op jit(solution)/shard_map/all_gather | solution.py:58
  15.5 7.3 %collective-permute-start = (bf16[128,256]{1,0:T(8,128)(2,1)S(1)}, bf16[128,256]{1,0:T(8,128)(2,1)S(1)}, u32[]{:S(2)}, u32[]{:S(2)}) collective-permute-start(bf16[128,256]{1,0:T(8,128)(2,1)S(1)} %convolution_convert_fusion.3), channel_id=1, source_target_pairs={{0,4},{4,8},{8,12},{12,0},{1,5},{5,9},{9,13},{13,1},{2,6},{6,10},{... | collective-permute-start | bytes 196616 | tf_op jit(solution)/shard_map/ppermute | solution.py:12
  22.9 6.1 %collective-permute-start.1 = (bf16[128,256]{1,0:T(8,128)(2,1)S(1)}, bf16[128,256]{1,0:T(8,128)(2,1)S(1)}, u32[]{:S(2)}, u32[]{:S(2)}) collective-permute-start(bf16[128,256]{1,0:T(8,128)(2,1)S(1)} %collective-permute-done), channel_id=1, source_target_pairs={{0,4},{4,8},{8,12},{12,0},{1,5},{5,9},{9,13},{13,1},{2,6},{6,10},{... | collective-permute-start | bytes 196616 | tf_op jit(solution)/shard_map/ppermute | solution.py:12
  29.0 6.1 %collective-permute-start.2 = (bf16[128,256]{1,0:T(8,128)(2,1)S(1)}, bf16[128,256]{1,0:T(8,128)(2,1)S(1)}, u32[]{:S(2)}, u32[]{:S(2)}) collective-permute-start(bf16[128,256]{1,0:T(8,128)(2,1)S(1)} %collective-permute-done.1), channel_id=1, source_target_pairs={{0,4},{4,8},{8,12},{12,0},{1,5},{5,9},{9,13},{13,1},{2,6},{6,10},{... | collective-permute-start | bytes 196616 | tf_op jit(solution)/shard_map/ppermute | solution.py:12
  35.9 0.7 copy-start.1
  36.6 71.7 %reduce-scatter.5.cloned.1.call-start = ((), (), s32[]{:S(2)}) async-start(), calls=%async_computation.4 | async-start | bytes 1966080 | tf_op jit(solution)/shard_map/reduce_scatter | solution.py:87
Sparse Core Ops, SparseCore 0:
  12.8 34.1 reduce-scatter.2
  49.1 16.8 all-gather.1
  82.4 25.9 reduce-scatter.4
